TPU v7x, 32 devices: a whole 2x2x4 slice. The times are simulated.
32 devices in a mesh: ctx: 8 (over y, x, core), head: 4 (over z).
Axes of the slice: x: 2, y: 2, z: 4, core: 2. Of those that a mesh axis runs over, the one named last changes fastest.
Arguments:
- tokens: int32 [2048], P('ctx'), may hold values from 0 to 4
- inputs: bfloat16 [2048, 4096], P('ctx', 'head'), may hold values from -6 to 6
- step_raw: float32 [64, 2048], P('head', 'ctx'), may hold values from -4 to 4
- step_bias: float32 [64], P('head'), may hold values from -1 to 1
- decay_log: float32 [64], P('head'), may hold values from -11 to -3.2
- skip_gain: float32 [64], P('head'), may hold values from 0.5 to 1.5
- bc_table: float32 [2, 5, 128], replicated, may hold values from -0.5 to 0.5
- features: bfloat16 [2048, 1024], P('ctx'), may hold values from -6 to 6
- bc_proj: bfloat16 [2, 1024, 128], replicated, may hold values from -0.01171875 to 0.01171875
- cotangent: bfloat16 [2048, 4096], P('ctx', 'head'), may hold values from -6 to 6
Outputs:
- mixed: bfloat16 [2048, 4096], P('ctx', 'head')
- input_grad: float32 [2048, 4096], P('ctx', 'head')
- step_grad: float32 [64, 2048], P('head', 'ctx')
- table_grad: float32 [2, 5, 128], replicated
- head_grads: float32 [3, 64], P(None, 'head')
- proj_grad: float32 [2, 1024, 128], replicated
All inputs are finite; a program needn't handle non-finite values.
Results may differ from a plain program's by a relative error of at most 0.001.
Values sent between devices are 32-bit elements; how exact they have to be, the bound alone decides.
A program may use at most 128 MiB of HBM per device.

v0:
```python
import functools

import jax
import jax.numpy as jnp
from jax import lax
from jax.experimental import pallas as pl
from jax.experimental.pallas import tpu as pltpu
from jax.sharding import PartitionSpec as P

f32, bf16 = jnp.float32, jnp.bfloat16
NN, NT, TN = ((1,), (0,)), ((1,), (1,)), ((0,), (0,))
COMP = (3, 2, 1, 0, 4)
PARAMS = dict(vmem_limit_bytes=50 * 1024 * 1024)


def dg(a, b, dims):
    return lax.dot_general(a, b, (dims, ((), ())), preferred_element_type=f32)


def split(v):
    hi = v.astype(bf16)
    return hi, (v - hi.astype(f32)).astype(bf16)


def mm2(exact, parts, dims):
    return dg(exact, parts[0], dims) + dg(exact, parts[1], dims)


def mm3(a, b, dims):
    return dg(a[0], b[0], dims) + dg(a[0], b[1], dims) + dg(a[1], b[0], dims)


def times_exact(v, exact, dims):
    hi, mid = split(v)
    low = (v - hi.astype(f32) - mid.astype(f32)).astype(bf16)
    return dg(hi, exact, dims) + dg(mid, exact, dims) + dg(low, exact, dims)


def softplus(v):
    return jnp.maximum(v, 0.0) + jnp.log1p(jnp.exp(-jnp.abs(v)))


def iotas(n):
    shape = (n, n)
    return lax.broadcasted_iota(jnp.int32, shape, 0), lax.broadcasted_iota(jnp.int32, shape, 1)


def flip_columns(feats):
    width = feats.shape[1]
    part = 256
    row, col = iotas(part)
    anti = (row + col == part - 1).astype(bf16)
    count = width // part
    return jnp.concatenate(
        [
            dg(feats[:, (count - 1 - k) * part : (count - k) * part], anti, NN).astype(bf16)
            for k in range(count)
        ],
        axis=1,
    )


def prep_kernel(
    tok_ref, x_ref, u_ref, step_ref, bias_ref, dlog_ref, table_ref, feat_ref, proj_ref,
    states_ref, rows_ref, bc_ref, xt_ref, ut_ref, flip_ref, tab, wide_hi, wide_lo,
):
    heads, length = step_ref.shape
    width = x_ref.shape[1] // heads
    delta = softplus(step_ref[...] + bias_ref[...])
    rate = -jnp.exp(dlog_ref[...]) * delta
    row, col = iotas(length)
    cum = times_exact(rate, (row <= col).astype(bf16), NN)
    total = cum[:, length - 1 : length]
    excl = cum - rate
    ef, wf = jnp.exp(cum), jnp.exp(total - cum) * delta
    er, wr = jnp.exp(total - excl), jnp.exp(excl) * delta
    for k, value in enumerate((cum, excl, delta, ef, wf, er, wr, rate)):
        for h in range(heads):
            rows_ref[h, k : k + 1, :] = value[h : h + 1, :]

    tab[...] = jnp.zeros_like(tab)
    tab[0:5, :] = table_ref[0]
    tab[8:13, :] = table_ref[1]
    kinds = lax.broadcasted_iota(jnp.int32, (8, length), 0)
    tok = tok_ref[...]
    hot = (kinds == tok).astype(bf16)
    hot_rev = (kinds == jnp.where(tok == 4, 4, 3 - tok)).astype(bf16)
    feats = feat_ref[...]
    flipped = flip_columns(feats)
    flip_ref[...] = flipped

    def look(onehot, table):
        hi, mid = split(table)
        low = (table - hi.astype(f32) - mid.astype(f32)).astype(bf16)
        return dg(onehot, hi, TN) + dg(onehot, mid, TN) + dg(onehot, low, TN)

    b_fwd = look(hot, tab[0:8, :]) + dg(feats, proj_ref[0], NN)
    c_fwd = look(hot, tab[8:16, :]) + dg(feats, proj_ref[1], NN)
    b_rev = look(hot_rev, tab[0:8, :]) + dg(flipped, proj_ref[0], NN)
    c_rev = look(hot_rev, tab[8:16, :]) + dg(flipped, proj_ref[1], NN)
    for k, value in enumerate((b_fwd, c_fwd, b_rev, c_rev)):
        bc_ref[k] = value

    xt_ref[...] = x_ref[...].astype(f32).T.astype(bf16)
    ut_ref[...] = u_ref[...].astype(f32).T.astype(bf16)
    plan = ((xt_ref, wf, b_fwd), (ut_ref, er, c_rev), (xt_ref, wr, b_rev), (ut_ref, ef, c_fwd))
    for k, (source, scale, right) in enumerate(plan):
        for h in range(heads):
            at = slice(h * width, (h + 1) * width)
            hi, lo = split(source[at, :].astype(f32) * scale[h : h + 1, :])
            wide_hi[at, :] = hi
            wide_lo[at, :] = lo
        states_ref[k] = mm3((wide_hi[...], wide_lo[...]), split(right), NN)


def intra_kernel(
    rows_ref, bc_ref, xt_ref, ut_ref, y_ref, dx_ref, sums_ref, dbc_ref, aff_f, aff_r, total
):
    length = xt_ref.shape[1]
    head = pl.program_id(0)
    row, col = iotas(length)

    @pl.when(head == 0)
    def _():
        b_fwd, c_fwd, b_rev, c_rev = [split(bc_ref[k]) for k in range(4)]
        aff_f[...] = jnp.where(col >= row, mm3(b_fwd, c_fwd, NT), 0.0)
        aff_r[...] = jnp.where(col <= row, mm3(b_rev, c_rev, NT), 0.0)
        total[...] = jnp.zeros_like(total)

    rows = rows_ref[0]
    cols = jnp.concatenate([rows, jnp.zeros((120, length), f32)], axis=0).T
    gap = jnp.where(
        col >= row, rows[0:1, :] - cols[:, 0:1], cols[:, 1:2] - rows[1:2, :]
    )
    decay = jnp.exp(gap) * cols[:, 2:3]
    xt, ut = xt_ref[...], ut_ref[...]
    total[...] += decay * dg(xt, ut, TN)
    v_fwd = split(decay * aff_f[...])
    v_rev = split(decay * aff_r[...])
    y_fwd, y_rev = mm2(xt, v_fwd, NN), mm2(xt, v_rev, NN)
    dx_fwd, dx_rev = mm2(ut, v_fwd, NT), mm2(ut, v_rev, NT)
    y_ref[...] = y_fwd + y_rev
    dx_ref[...] = dx_fwd + dx_rev
    xw, uw = xt.astype(f32), ut.astype(f32)
    sums_ref[0, 0:1, :] = jnp.sum(uw * y_fwd, axis=0, keepdims=True)
    sums_ref[0, 1:2, :] = jnp.sum(uw * y_rev, axis=0, keepdims=True)
    sums_ref[0, 2:3, :] = jnp.sum(xw * dx_fwd, axis=0, keepdims=True)
    sums_ref[0, 3:4, :] = jnp.sum(xw * dx_rev, axis=0, keepdims=True)
    sums_ref[0, 4:5, :] = jnp.sum(xw * uw, axis=0, keepdims=True)

    @pl.when(head == pl.num_programs(0) - 1)
    def _():
        grads = total[...]
        b_fwd, c_fwd, b_rev, c_rev = [split(bc_ref[k]) for k in range(4)]
        g_fwd = split(jnp.where(col >= row, grads, 0.0))
        g_rev = split(jnp.where(col <= row, grads, 0.0))
        dbc_ref[0] = mm3(g_fwd, c_fwd, NN)
        dbc_ref[1] = mm3(g_fwd, b_fwd, TN)
        dbc_ref[2] = mm3(g_rev, c_rev, NN)
        dbc_ref[3] = mm3(g_rev, b_rev, TN)


def finish_kernel(
    tok_ref, step_ref, bias_ref, dlog_ref, gain_ref, rows_ref, sums_ref, bc_ref, dbc_ref,
    xt_ref, ut_ref, y_ref, dx_ref, in_ref, feat_ref, flip_ref,
    mixed_ref, igrad_ref, sgrad_ref, tgrad_ref, hgrad_ref, pgrad_ref,
    inter, wide_hi, wide_lo, heads_scr, const_scr,
):
    heads, length = step_ref.shape
    width = xt_ref.shape[0] // heads
    plan = ((0, 1, 3, ut_ref), (2, 3, 5, ut_ref), (3, 0, 4, xt_ref), (1, 2, 6, xt_ref))
    grads = [None] * 4
    for k, (state, right, scale, source) in enumerate(plan):
        parts = split(in_ref[state])
        inter[k] = mm3(parts, split(bc_ref[right]), NT)
        for h in range(heads):
            at = slice(h * width, (h + 1) * width)
            hi, lo = split(source[at, :].astype(f32) * rows_ref[h, scale : scale + 1, :])
            wide_hi[at, :] = hi
            wide_lo[at, :] = lo
        got = mm3(parts, (wide_hi[...], wide_lo[...]), TN)
        grads[right] = dbc_ref[right] + got.T

    for pair in range(heads // 2):
        ys, dxs = [], []
        for h in (2 * pair, 2 * pair + 1):
            at = slice(h * width, (h + 1) * width)
            xw, uw = xt_ref[at, :].astype(f32), ut_ref[at, :].astype(f32)
            gain = gain_ref[h : h + 1, :]
            y_fwd = inter[0, at, :] * rows_ref[h, 3:4, :]
            y_rev = inter[1, at, :] * rows_ref[h, 5:6, :]
            dx_fwd = inter[2, at, :] * rows_ref[h, 4:5, :]
            dx_rev = inter[3, at, :] * rows_ref[h, 6:7, :]
            ys.append(y_ref[at, :] + y_fwd + y_rev + gain * xw)
            dxs.append(dx_ref[at, :] + dx_fwd + dx_rev + gain * uw)
            a_fwd = jnp.sum(uw * y_fwd, axis=0, keepdims=True)
            a_rev = jnp.sum(uw * y_rev, axis=0, keepdims=True)
            q_fwd = jnp.sum(xw * dx_fwd, axis=0, keepdims=True)
            q_rev = jnp.sum(xw * dx_rev, axis=0, keepdims=True)
            heads_scr[0, h : h + 1, :] = sums_ref[h, 0:1, :] + a_fwd
            heads_scr[1, h : h + 1, :] = sums_ref[h, 1:2, :] + a_rev
            heads_scr[2, h : h + 1, :] = sums_ref[h, 2:3, :] + q_fwd
            heads_scr[3, h : h + 1, :] = sums_ref[h, 3:4, :] + q_rev
            heads_scr[4, h : h + 1, :] = sums_ref[h, 4:5, :]
            heads_scr[5, h : h + 1, :] = q_fwd + q_rev
            cross = in_ref[0, at, :] * in_ref[3, at, :] + in_ref[1, at, :] * in_ref[2, at, :]
            const_scr[h : h + 1, :] = jnp.sum(cross, axis=0, keepdims=True)
        lanes = slice(pair * 2 * width, (pair + 1) * 2 * width)
        mixed_ref[:, lanes] = jnp.concatenate(ys, axis=0).T.astype(bf16)
        igrad_ref[:, lanes] = jnp.concatenate(dxs, axis=0).T

    raw = step_ref[...] + bias_ref[...]
    delta = softplus(raw)
    mag = jnp.exp(dlog_ref[...])
    rate = -mag * delta
    row, col = iotas(length)
    after = (row >= col).astype(bf16)
    before = (row <= col).astype(bf16)
    z_fwd = heads_scr[0] - heads_scr[2]
    z_rev = heads_scr[1] - heads_scr[3]
    decay_all = jnp.exp(jnp.sum(rate, axis=1, keepdims=True))
    const = decay_all * jnp.sum(const_scr[...], axis=1, keepdims=True) + jnp.sum(
        heads_scr[5], axis=1, keepdims=True
    )
    rate_grad = times_exact(z_fwd, after, NN) + times_exact(z_rev, before, NN) + const
    delta_grad = (heads_scr[2] + heads_scr[3]) / delta - mag * rate_grad
    step_grad = delta_grad / (1.0 + jnp.exp(-raw))
    sgrad_ref[...] = step_grad
    hgrad_ref[...] = jnp.zeros_like(hgrad_ref)
    hgrad_ref[:, 0:1] = jnp.sum(rate_grad * rate, axis=1, keepdims=True)
    hgrad_ref[:, 1:2] = jnp.sum(step_grad, axis=1, keepdims=True)
    hgrad_ref[:, 2:3] = jnp.sum(heads_scr[4], axis=1, keepdims=True)

    tok = tok_ref[...]
    kinds = lax.broadcasted_iota(jnp.int32, (8, length), 0)
    hot = (kinds == tok).astype(bf16)
    hot_rev = (kinds == jnp.where(tok == 4, 4, 3 - tok)).astype(bf16)
    parts = [split(g) for g in grads]
    for k in range(2):
        fwd, rev = parts[k], parts[2 + k]
        tgrad_ref[k] = (mm2(hot, fwd, NN) + mm2(hot_rev, rev, NN))[0:5, :]
        pgrad_ref[k] = mm2(feat_ref[...], fwd, TN) + mm2(flip_ref[...], rev, TN)


def call(kernel, outs, scratch, cost=None, **kwargs):
    return pl.pallas_call(
        kernel,
        out_shape=[jax.ShapeDtypeStruct(shape, dtype) for shape, dtype in outs],
        scratch_shapes=[pltpu.VMEM(shape, dtype) for shape, dtype in scratch],
        compiler_params=pltpu.CompilerParams(**PARAMS),
        cost_estimate=cost,
        **kwargs,
    )


def scan_gather(states, decays):
    count, mine = lax.axis_size("ctx"), lax.axis_index("ctx")
    pieces = lax.all_gather(states, "ctx")

    def step(j, sums):
        up, down = sums
        back = count - 1 - j
        longer_up = up * decays[j][:, None] + pieces[j, :2]
        longer_down = down * decays[back][:, None] + pieces[back, 2:]
        return jnp.where(j < mine, longer_up, up), jnp.where(back > mine, longer_down, down)

    zero = jnp.zeros_like(states[:2])
    up, down = lax.fori_loop(0, count - 1, step, (zero, zero))
    return jnp.concatenate([up, down], axis=0)


def scan_pairs(states, decays):
    count, mine = lax.axis_size("ctx"), lax.axis_index("ctx")
    core, pair = mine % 2, mine // 2
    pairs = count // 2
    half = states.shape[1] // 2
    swap = [(i, i ^ 1) for i in range(count)]
    halves = states.reshape(4, 2, half, states.shape[2])
    first = core == 0
    own = jnp.where(first, halves[:, 0], halves[:, 1])
    got = lax.ppermute(jnp.where(first, halves[:, 1], halves[:, 0]), "ctx", swap)
    low, high = jnp.where(first, own, got), jnp.where(first, got, own)
    decays = lax.dynamic_slice_in_dim(decays, core * half, half, 1)
    by_pair = decays.reshape(pairs, 2, half)
    both = by_pair[:, 0] * by_pair[:, 1]
    dec_low = lax.dynamic_index_in_dim(by_pair[:, 0], pair, 0, False)[:, None]
    dec_high = lax.dynamic_index_in_dim(by_pair[:, 1], pair, 0, False)[:, None]
    up = low[:2] * dec_high + high[:2]
    down = high[2:] * dec_low + low[2:]
    index = jnp.arange(pairs)[:, None]
    sum_up, sum_down = 0.0, 0.0
    for k in range(1, pairs):
        other = pair ^ k
        moves = [(i, i ^ (2 * k)) for i in range(count)]
        piece = lax.ppermute(jnp.where(other > pair, up, down), "ctx", moves)
        between = (index > jnp.minimum(pair, other)) & (index < jnp.maximum(pair, other))
        factor = jnp.prod(jnp.where(between, both, 1.0), axis=0)[:, None]
        sum_up += piece * jnp.where(other < pair, factor, 0.0)
        sum_down += piece * jnp.where(other > pair, factor, 0.0)
    for_low = jnp.concatenate([sum_up, sum_down * dec_high + high[2:]], axis=0)
    for_high = jnp.concatenate([sum_up * dec_low + low[:2], sum_down], axis=0)
    keep = jnp.where(first, for_low, for_high)
    other_half = lax.ppermute(jnp.where(first, for_high, for_low), "ctx", swap)
    return jnp.concatenate(
        [jnp.where(first, keep, other_half), jnp.where(first, other_half, keep)], axis=1
    )


def body(
    tokens, inputs, step_raw, step_bias, decay_log, skip_gain, bc_table, features, bc_proj, cotangent
):
    heads, length = step_raw.shape
    wide = inputs.shape[1]
    width = wide // heads
    feat, state = bc_proj.shape[1:]
    tok = tokens.reshape(1, length)
    bias, logs, gain = (v.reshape(heads, 1) for v in (step_bias, decay_log, skip_gain))
    totals = -jnp.exp(decay_log) * jnp.sum(jax.nn.softplus(step_raw + bias), axis=1)
    decays = jnp.exp(jnp.repeat(lax.all_gather(totals, "ctx"), width, axis=1))

    states, rows, bc, xt, ut, flipped = call(
        prep_kernel,
        [
            ((4, wide, state), f32),
            ((heads, 8, length), f32),
            ((4, length, state), f32),
            ((wide, length), bf16),
            ((wide, length), bf16),
            ((length, feat), bf16),
        ],
        [((16, state), f32), ((wide, length), bf16), ((wide, length), bf16)],
    )(tok, inputs, cotangent, step_raw, bias, logs, bc_table, features, bc_proj)

    count = lax.axis_size("ctx")
    paired = count <= 16 and count & (count - 1) == 0 and count > 2 and heads % 2 == 0
    incoming = (scan_pairs if paired else scan_gather)(states, decays)

    per_head = pl.BlockSpec((width, length), lambda h: (h, 0))
    per_rows = pl.BlockSpec((1, 8, length), lambda h: (h, 0, 0))
    whole = pl.BlockSpec((4, length, state), lambda h: (0, 0, 0))
    y, dx, sums, dbc = call(
        intra_kernel,
        [
            ((wide, length), f32),
            ((wide, length), f32),
            ((heads, 8, length), f32),
            ((4, length, state), f32),
        ],
        [((length, length), f32)] * 3,
        pl.CostEstimate(
            flops=heads * length * length * width * 18,
            bytes_accessed=wide * length * 12,
            transcendentals=heads * length * length,
        ),
        grid=(heads,),
        in_specs=[per_rows, whole, per_head, per_head],
        out_specs=[per_head, per_head, per_rows, whole],
    )(rows, bc, xt, ut)

    mixed, input_grad, step_grad, table_local, head_local, proj_local = call(
        finish_kernel,
        [
            ((length, wide), bf16),
            ((length, wide), f32),
            ((heads, length), f32),
            ((2, 5, state), f32),
            ((heads, 128), f32),
            ((2, feat, state), f32),
        ],
        [
            ((4, wide, length), f32),
            ((wide, length), bf16),
            ((wide, length), bf16),
            ((6, heads, length), f32),
            ((heads, state), f32),
        ],
    )(
        tok, step_raw, bias, logs, gain, rows, sums, bc, dbc, xt, ut, y, dx, incoming, features, flipped
    )
    table_grad, proj_grad = lax.psum((table_local, proj_local), ("ctx", "head"))
    head_grads = lax.psum(head_local[:, :3].T, "ctx")
    return mixed, input_grad, step_grad, table_grad, head_grads, proj_grad


def solution(mesh):
    in_specs = (
        P("ctx"),
        P("ctx", "head"),
        P("head", "ctx"),
        P("head"),
        P("head"),
        P("head"),
        P(),
        P("ctx", None),
        P(),
        P("ctx", "head"),
    )
    out_specs = (P("ctx", "head"), P("ctx", "head"), P("head", "ctx"), P(), P(None, "head"), P())
    return jax.shard_map(body, mesh=mesh, in_specs=in_specs, out_specs=out_specs, check_vma=False)
```

profile of v0, /device:TPU:0, one launch (start us, length us, event | category | flops | bytes accessed | tf_op | source)
XLA Modules:
  0.0 231.5 jit_solution(12546946588684155086)
XLA Ops:
  7.2 0.0 all-reduce.3.cloned.1.call-start
  7.2 0.7 copy.50.dlog_ref
  8.0 0.7 copy.49.bias_ref
  8.7 0.7 copy.46.table_ref
  9.4 1.0 copy-done
  10.4 1.0 copy-done.3
  11.5 1.0 copy-done.4
  12.5 0.7 copy-done.5
  13.2 0.7 copy-done.7
  13.9 5.3 %shard_map.145 = (f32[4,1024,128]{2,1,0:T(8,128)}, f32[16,8,256]{2,1,0:T(8,128)S(1)}, f32[4,256,128]{2,1,0:T(8,128)S(1)}, bf16[1024,256]{1,0:T(8,128)(2,1)S(1)},...) custom-call(s32[1,256]{1,0:T(1,128)S(1)} %bitcast.45, bf16[256,1024]{1,0:T(8,128)(2,1)S(1)} %copy-done.3, ...), custom_call_target="tpu_custom_call" | custom-call | tf_op jit(solution)/shard_map/pallas_call | solution.py:321
  19.2 1.7 select_bitcast_fusion
  20.9 0.5 collective-permute-start
  21.5 0.2 fusion.3
  21.7 0.6 dynamic-slice.2
  23.0 0.1 multiply_dynamic-update-slice_fusion
  23.1 15.3 %all-reduce = f32[128]{0:T(128)S(1)} all-reduce(f32[128]{0:T(128)S(1)} %multiply_dynamic-update-slice_fusion), channel_id=2, replica_groups=mesh['ctx'=8,'head'=4] {'ctx'}, use_global_device_ids=true, to_apply=%add | all-reduce | flops 128 | bytes 1024
  38.4 0.1 reshape.116
  38.5 0.1 broadcast_in_dim.46
  38.6 0.1 exp.17
  38.8 2.0 bitcast_select_fusion.1
  40.9 0.2 broadcast_select_fusion.4
  41.1 0.1 collective-permute-start.1
  41.2 0.1 broadcast_select_fusion.3
  41.2 0.6 collective-permute-start.2
  41.8 3.0 %collective-permute-start.3 = (f32[2,512,128]{2,1,0:T(8,128)S(1)}, f32[2,512,128]{2,1,0:T(8,128)S(1)}, u32[]{:S(2)}, u32[]{:S(2)}) collective-permute-start(f32[2,512,128]{2,1,0:T(8,128)S(1)} %get-tuple-element.79), channel_id=1, source_target_pairs={{0,24},{4,28},{8,16},{12,20},{16,8},{20,12},{24,0},{28,4},{1,25},{... | collective-permute-start | bytes 1572872 | tf_op jit(solution)/shard_map/ppermute | solution.py:295
  44.8 0.1 fusion.4
  44.9 11.1 %collective-permute-done.1 = f32[2,512,128]{2,1,0:T(8,128)S(1)} collective-permute-done((f32[2,512,128]{2,1,0:T(8,128)S(1)}, f32[2,512,128]{2,1,0:T(8,128)S(1)}, u32[]{:S(2)}, u32[]{:S(2)}) %collective-permute-start.1) | collective-permute-done | bytes 524320 | tf_op jit(solution)/shard_map/ppermute | solution.py:295
  56.0 9.0 %collective-permute-done.2 = f32[2,512,128]{2,1,0:T(8,128)S(1)} collective-permute-done((f32[2,512,128]{2,1,0:T(8,128)S(1)}, f32[2,512,128]{2,1,0:T(8,128)S(1)}, u32[]{:S(2)}, u32[]{:S(2)}) %collective-permute-start.2) | collective-permute-done | bytes 524320 | tf_op jit(solution)/shard_map/ppermute | solution.py:295
  65.0 0.0 collective-permute-done.3
  65.0 0.8 multiply_add_fusion
  65.8 0.0 copy-start.11
  65.8 0.0 copy-start.15
  65.8 1.3 fusion.1
  67.1 0.1 copy.51.gain_ref
  67.2 13.3 %shard_map.146 = (f32[1024,256]{1,0:T(8,128)S(1)}, f32[1024,256]{1,0:T(8,128)}, f32[16,8,256]{2,1,0:T(8,128)S(1)}, f32[4,256,128]{2,1,0:T(8,128)S(1)}) custom-call(f32[16,8,256]{2,1,0:T(8,128)S(1)} %get-tuple-element.22.rows_ref, f32[4,256,128]{2,1,0:T(8,128)S(1)} %get-tuple-element.23.bc_ref, bf16[1024,256]{1,0:T(8,128)(2,1)S(1)} %get-tuple-element.24.xt_ref, ...), custom_call_target="tpu_custom_call" | custom-call | flops 1207959552 | bytes 3145728 | tf_op jit(solution)/shard_map/pallas_call | solution.py:341
  80.5 1.8 broadcast_select_fusion.1
  82.3 0.0 copy-start.1
  82.4 0.0 copy-start.6
  82.4 0.0 copy-start.8
  82.4 1.5 pad_maximum_fusion.in_ref
  83.9 7.9 %shard_map.147 = (bf16[256,1024]{1,0:T(8,128)(2,1)}, f32[256,1024]{1,0:T(8,128)}, f32[16,256]{1,0:T(8,128)}, f32[2,5,128]{2,1,0:T(8,128)S(1)}, f32[16,128]{1,0:T(8,128)S(1)}, /*index=5*/f32[2,1024,128]{2,1,0:T(8,128)}) custom-call(s32[1,256]{1,0:T(1,128)S(1)} %bitcast.46, f32[16,256]{1,0:T(8,128)S(1)} %copy-done.6, f32[16,1]{1,0:T(8,128)S(1)} %copy.49.bias_ref, ...), custom_call_target="tpu_custom_call" | custom-call | tf_op jit(solution)/shard_map/pallas_call | solution.py:360
  91.8 0.0 all-reduce.3.cloned.1.call-update
  91.8 39.8 %psum.21 = f32[2,5,128]{2,1,0:T(8,128)S(1)} all-reduce(f32[2,5,128]{2,1,0:T(8,128)S(1)} %get-tuple-element.35), channel_id=1, replica_groups=mesh['ctx'=8,'head'=4] {'ctx','head'}, use_global_device_ids=true, to_apply=%region_4.5 | all-reduce | flops 1280 | bytes 10240 | tf_op jit(solution)/shard_map/psum | solution.py:380
  131.6 0.6 copy.52
  132.2 13.0 %psum.22 = f32[3,16]{0,1:T(8,128)S(1)} all-reduce(f32[3,16]{0,1:T(8,128)S(1)} %slice_bitcast_fusion.2), channel_id=1, replica_groups=mesh['ctx'=8,'head'=4] {'ctx'}, use_global_device_ids=true, to_apply=%region_5.6 | all-reduce | flops 48 | bytes 384 | tf_op jit(solution)/shard_map/psum | solution.py:381
  145.2 0.7 copy.53
  145.8 76.6 %all-reduce.3.cloned.1.call-done = f32[2,1024,128]{2,1,0:T(8,128)} async-done(((f32[2,1024,128]{2,1,0:T(8,128)}), f32[2,1024,128]{2,1,0:T(8,128)}) %all-reduce.3.cloned.1.call-update) | async-done | bytes 1048592 | tf_op jit(solution)/shard_map/psum | solution.py:380
  222.4 2.3 copy.62
  (39 shorter events, 0.1 us)
Async XLA Ops:
  7.2 215.2 %all-reduce.3.cloned.1.call-start = ((), (), s32[]{:S(2)}) async-start(), calls=%async_computation | async-start | bytes 2097152 | tf_op jit(solution)/shard_map/psum | solution.py:380
  9.4 1.0 copy-start
  10.4 1.0 copy-start.3
  11.5 1.0 copy-start.4
  12.5 0.7 copy-start.5
  13.2 0.7 copy-start.7
  19.2 2.2 copy-start.13
  19.2 2.5 %copy-start.16 = (u32[32]{0:T(128)S(1)}, u32[32]{0:T(128)}, u32[]{:S(2)}) copy-start(u32[32]{0:T(128)} %constant.55) | copy-start | bytes 388
  19.2 3.7 %copy-start.14 = (f32[16]{0:T(128)S(1)}, f32[16]{0:T(128)}, u32[]{:S(2)}) copy-start(f32[16]{0:T(128)} %param.14) | copy-start | bytes 196
  20.9 17.9 %collective-permute-start = (f32[4,512,128]{2,1,0:T(8,128)S(1)}, f32[4,512,128]{2,1,0:T(8,128)}, u32[]{:S(2)}, u32[]{:S(2)}) collective-permute-start(f32[4,512,128]{2,1,0:T(8,128)S(1)} %select_bitcast_fusion), channel_id=1, source_target_pairs={{0,4},{4,0},{8,12},{12,8},{16,20},{20,16},{24,28},{28,24},{1,5},{5... | collective-permute-start | bytes 3145736 | tf_op jit(solution)/shard_map/ppermute | solution.py:281
  41.1 14.9 %collective-permute-start.1 = (f32[2,512,128]{2,1,0:T(8,128)S(1)}, f32[2,512,128]{2,1,0:T(8,128)S(1)}, u32[]{:S(2)}, u32[]{:S(2)}) collective-permute-start(f32[2,512,128]{2,1,0:T(8,128)S(1)} %get-tuple-element.69), channel_id=1, source_target_pairs={{0,8},{4,12},{8,0},{12,4},{16,24},{20,28},{24,16},{28,20},{1,9},{5... | collective-permute-start | bytes 1572872 | tf_op jit(solution)/shard_map/ppermute | solution.py:295
  41.2 23.7 %collective-permute-start.2 = (f32[2,512,128]{2,1,0:T(8,128)S(1)}, f32[2,512,128]{2,1,0:T(8,128)S(1)}, u32[]{:S(2)}, u32[]{:S(2)}) collective-permute-start(f32[2,512,128]{2,1,0:T(8,128)S(1)} %get-tuple-element.78), channel_id=1, source_target_pairs={{0,16},{4,20},{8,24},{12,28},{16,0},{20,4},{24,8},{28,12},{1,17},{... | collective-permute-start | bytes 1572872 | tf_op jit(solution)/shard_map/ppermute | solution.py:295
  41.8 23.2 %collective-permute-start.3 = (f32[2,512,128]{2,1,0:T(8,128)S(1)}, f32[2,512,128]{2,1,0:T(8,128)S(1)}, u32[]{:S(2)}, u32[]{:S(2)}) collective-permute-start(f32[2,512,128]{2,1,0:T(8,128)S(1)} %get-tuple-element.79), channel_id=1, source_target_pairs={{0,24},{4,28},{8,16},{12,20},{16,8},{20,12},{24,0},{28,4},{1,25},{... | collective-permute-start | bytes 1572872 | tf_op jit(solution)/shard_map/ppermute | solution.py:295
  65.8 1.3 copy-start.9
  65.8 1.3 copy-start.11
  65.8 1.3 copy-start.15
  67.1 13.4 %collective-permute-start.4 = (f32[4,512,128]{2,1,0:T(8,128)}, f32[4,512,128]{2,1,0:T(8,128)}, u32[]{:S(2)}, u32[]{:S(2)}) collective-permute-start(f32[4,512,128]{2,1,0:T(8,128)} %fusion.1), channel_id=1, source_target_pairs={{0,4},{4,0},{8,12},{12,8},{16,20},{20,16},{24,28},{28,24},{1,5},{5... | collective-permute-start | bytes 3145736 | tf_op jit(solution)/shard_map/ppermute | solution.py:303
  67.2 13.3 %copy-start.10 = (f32[2,512,128]{2,1,0:T(8,128)S(1)}, f32[2,512,128]{2,1,0:T(8,128)}, u32[]{:S(2)}) copy-start(f32[2,512,128]{2,1,0:T(8,128)} %copy-done.9) | copy-start | bytes 1572868
  67.2 13.3 %copy-start.12 = (f32[2,512,128]{2,1,0:T(8,128)S(1)}, f32[2,512,128]{2,1,0:T(8,128)}, u32[]{:S(2)}) copy-start(f32[2,512,128]{2,1,0:T(8,128)} %copy-done.11) | copy-start | bytes 1572868
  80.5 1.9 copy-start.2
  82.3 1.5 copy-start.1
  82.4 1.5 copy-start.6
  82.4 1.5 copy-start.8
Sparse Core Ops, SparseCore 0:
  91.9 130.4 all-reduce.2
where the time goes:
time: 232 us; the launch traced here: 231 us
  waiting for transfers between devices  96.7 us (42%)
  blocking collectives  68.1 us (29%)
  Pallas kernels  26.5 us (11%)
  between operations  15 us (6%)
  local copies, waits for them, and re-layouts  11.2 us (5%)
  other arithmetic  9.83 us (4%)
  starting transfers between devices  4.17 us (2%)
    psum x1, waiting for transfers between devices, body(): table_grad, proj_grad = lax.psum((table_local, proj_local), ('ctx', 'head'))  76.6 us
    psum x1, blocking collectives, body(): table_grad, proj_grad = lax.psum((table_local, proj_local), ('ctx', 'head'))  39.8 us
    ppermute x3, waiting for transfers between devices, scan_pairs(): piece = lax.ppermute(jnp.where(other > pair, up, down), 'ctx', moves)  20.1 us
    unnamed x1, blocking collectives  15.3 us
    pallas_call x1, Pallas kernels, body(): call(intra_kernel, [((wide, length), f32), ((wide, length), f32), ((heads...  13.3 us
    psum x1, blocking collectives, body(): head_grads = lax.psum(head_local[:, :3].T, 'ctx')  13 us
    unnamed x40, local copies, waits for them, and re-layouts  9.36 us
    pallas_call x1, Pallas kernels, body(): call(finish_kernel, [((length, wide), bf16), ((length, wide), f32), ((hea...  7.9 us
  transfers between devices with their start and end apart: 6, of which 3 were waited for; matrix products, arithmetic and copies ran while one was open for 1% of the time, Pallas kernels for 6%

commit v1 on v0

--- a/solution.py
+++ b/solution.py
@@ -163,7 +163,7 @@
 def finish_kernel(
     tok_ref, step_ref, bias_ref, dlog_ref, gain_ref, rows_ref, sums_ref, bc_ref, dbc_ref,
     xt_ref, ut_ref, y_ref, dx_ref, in_ref, feat_ref, flip_ref,
-    mixed_ref, igrad_ref, sgrad_ref, tgrad_ref, hgrad_ref, pgrad_ref,
+    mixed_ref, igrad_ref, sgrad_ref, sum_ref,
     inter, wide_hi, wide_lo, heads_scr, const_scr,
 ):
     heads, length = step_ref.shape
@@ -226,10 +226,12 @@
     delta_grad = (heads_scr[2] + heads_scr[3]) / delta - mag * rate_grad
     step_grad = delta_grad / (1.0 + jnp.exp(-raw))
     sgrad_ref[...] = step_grad
-    hgrad_ref[...] = jnp.zeros_like(hgrad_ref)
-    hgrad_ref[:, 0:1] = jnp.sum(rate_grad * rate, axis=1, keepdims=True)
-    hgrad_ref[:, 1:2] = jnp.sum(step_grad, axis=1, keepdims=True)
-    hgrad_ref[:, 2:3] = jnp.sum(heads_scr[4], axis=1, keepdims=True)
+    feat = feat_ref.shape[1]
+    sum_ref[2 * feat :, :] = jnp.zeros((sum_ref.shape[0] - 2 * feat, sum_ref.shape[1]), f32)
+    mine = pl.ds(2 * feat + 16 + lax.axis_index("head") * heads, heads)
+    sum_ref[mine, 0:1] = jnp.sum(rate_grad * rate, axis=1, keepdims=True)
+    sum_ref[mine, 1:2] = jnp.sum(step_grad, axis=1, keepdims=True)
+    sum_ref[mine, 2:3] = jnp.sum(heads_scr[4], axis=1, keepdims=True)
 
     tok = tok_ref[...]
     kinds = lax.broadcasted_iota(jnp.int32, (8, length), 0)
@@ -238,8 +240,111 @@
     parts = [split(g) for g in grads]
     for k in range(2):
         fwd, rev = parts[k], parts[2 + k]
-        tgrad_ref[k] = (mm2(hot, fwd, NN) + mm2(hot_rev, rev, NN))[0:5, :]
-        pgrad_ref[k] = mm2(feat_ref[...], fwd, TN) + mm2(flip_ref[...], rev, TN)
+        at = 2 * feat + 5 * k
+        sum_ref[at : at + 5, :] = (mm2(hot, fwd, NN) + mm2(hot_rev, rev, NN))[0:5, :]
+        sum_ref[k * feat : (k + 1) * feat, :] = mm2(feat_ref[...], fwd, TN) + mm2(
+            flip_ref[...], rev, TN
+        )
+
+
+def remote(src, dst, send, recv, ctx, head):
+    return pltpu.make_async_remote_copy(
+        src_ref=src,
+        dst_ref=dst,
+        send_sem=send,
+        recv_sem=recv,
+        device_id=(ctx, head),
+        device_id_type=pl.DeviceIdType.MESH,
+    )
+
+
+def greet(peers):
+    barrier = pltpu.get_barrier_semaphore()
+    for peer in peers:
+        pl.semaphore_signal(
+            barrier, inc=1, device_id=peer, device_id_type=pl.DeviceIdType.MESH
+        )
+    pl.semaphore_wait(barrier, len(peers))
+
+
+def reduce_kernel(
+    part_ref, proj_ref, table_ref, heads_ref, out, acc, got1, got2, got3, gotz, send, recv, sendz, recvz
+):
+    ctx, head = lax.axis_index("ctx"), lax.axis_index("head")
+    bits = (ctx % 2, (ctx // 2) % 2, ctx // 4)
+    partners = [ctx + (1 - 2 * bit) * stride for bit, stride in zip(bits, (1, 2, 4))]
+    others = [lax.rem(head + d, 4) for d in (1, 2, 3)]
+    greet([(p, head) for p in partners] + [(ctx, o) for o in others])
+    start, size = 0, part_ref.shape[0]
+    kept = []
+    for i, (bit, partner, got) in enumerate(zip(bits, partners, (got1, got2, got3))):
+        size //= 2
+        keep = pl.ds(pl.multiple_of(start + bit * size, 8), size)
+        give = pl.ds(pl.multiple_of(start + (1 - bit) * size, 8), size)
+        source = part_ref if i == 0 else acc
+        copy = remote(source.at[give], got, send.at[i], recv.at[i], partner, head)
+        copy.start()
+        copy.wait()
+        acc[keep, :] = source[keep, :] + got[...]
+        kept.append(keep)
+        start = start + bit * size
+    size //= 4
+    quarter = lambda z: pl.ds(pl.multiple_of(start + z * size, 8), size)
+    copies = [
+        remote(acc.at[quarter(o)], gotz.at[d], sendz.at[d], recvz.at[d], ctx, o)
+        for d, o in enumerate(others)
+    ]
+    for copy in copies:
+        copy.start()
+    for copy in copies:
+        copy.wait()
+    mine = quarter(head)
+    out[mine, :] = acc[mine, :] + gotz[0] + gotz[1] + gotz[2]
+    copies = [
+        remote(out.at[mine], out.at[mine], sendz.at[3 + d], recvz.at[3 + d], ctx, o)
+        for d, o in enumerate(others)
+    ]
+    for copy in copies:
+        copy.start()
+    for copy in copies:
+        copy.wait()
+    for i in (2, 1, 0):
+        copy = remote(
+            out.at[kept[i]], out.at[kept[i]], send.at[3 + i], recv.at[3 + i], partners[i], head
+        )
+        copy.start()
+        copy.wait()
+    feat, heads = proj_ref.shape[1], heads_ref.shape[0]
+    for k in range(2):
+        proj_ref[k] = out[k * feat : (k + 1) * feat, :]
+        table_ref[k] = out[2 * feat + 5 * k : 2 * feat + 5 * k + 5, :]
+    heads_ref[...] = out[pl.ds(pl.multiple_of(2 * feat + 16 + head * heads, 8), heads), :]
+
+
+def reduce_all(part, feat, heads):
+    rows, state = part.shape
+    shapes = [(2, feat, state), (2, 5, state), (heads, state)]
+    if lax.axis_size("ctx") == 8 and lax.axis_size("head") == 4 and heads % 8 == 0:
+        return pl.pallas_call(
+            reduce_kernel,
+            out_shape=[jax.ShapeDtypeStruct(shape, f32) for shape in shapes],
+            scratch_shapes=[
+                pltpu.VMEM((rows // cut, state), f32) for cut in (1, 1, 2, 4, 8)
+            ]
+            + [pltpu.VMEM((3, rows // 32, state), f32)]
+            + [pltpu.SemaphoreType.DMA((6,))] * 4,
+            in_specs=[pl.BlockSpec(memory_space=pltpu.VMEM)],
+            compiler_params=pltpu.CompilerParams(
+                collective_id=0, has_side_effects=True, **PARAMS
+            ),
+        )(part)
+    total = lax.psum(part, ("ctx", "head"))
+    at = 2 * feat + 16 + lax.axis_index("head") * heads
+    return (
+        total[: 2 * feat].reshape(shapes[0]),
+        total[2 * feat : 2 * feat + 10].reshape(shapes[1]),
+        lax.dynamic_slice_in_dim(total, at, heads, 0),
+    )
 
 
 def call(kernel, outs, scratch, cost=None, **kwargs):
@@ -357,15 +462,14 @@
         out_specs=[per_head, per_head, per_rows, whole],
     )(rows, bc, xt, ut)
 
-    mixed, input_grad, step_grad, table_local, head_local, proj_local = call(
+    sum_rows = 2 * feat + 16 + heads * lax.axis_size("head")
+    mixed, input_grad, step_grad, local_sums = call(
         finish_kernel,
         [
             ((length, wide), bf16),
             ((length, wide), f32),
             ((heads, length), f32),
-            ((2, 5, state), f32),
-            ((heads, 128), f32),
-            ((2, feat, state), f32),
+            ((pl.cdiv(sum_rows, 256) * 256, state), f32),
         ],
         [
             ((4, wide, length), f32),
@@ -377,8 +481,8 @@
     )(
         tok, step_raw, bias, logs, gain, rows, sums, bc, dbc, xt, ut, y, dx, incoming, features, flipped
     )
-    table_grad, proj_grad = lax.psum((table_local, proj_local), ("ctx", "head"))
-    head_grads = lax.psum(head_local[:, :3].T, "ctx")
+    proj_grad, table_grad, head_sums = reduce_all(local_sums, feat, heads)
+    head_grads = head_sums[:, :3].T
     return mixed, input_grad, step_grad, table_grad, head_grads, proj_grad
 
 

time: 232 us -> 128 us (0.55)
  waiting for transfers between devices: 96.7 us -> 20.1 us
  blocking collectives: 68.1 us -> 15.3 us
  Pallas kernels: 26.5 us -> 65.8 us
  between operations: 15 us -> 1.61 us
    psum x1 -> x0, waiting for transfers between devices: 76.6 us -> none  [body(): table_grad, proj_grad = lax.psum((table_local, proj_local), ('ctx', 'head'))]
    psum x2 -> x0, blocking collectives: 52.8 us -> none  [the longest x1 39.8 us: body(): table_grad, proj_grad = lax.psum((table_local, proj_local), ('ctx', 'head'))]
    pallas_call x0 -> x1, Pallas kernels: none -> 39.2 us  [reduce_all(): pl.pallas_call(reduce_kernel, out_shape=[jax.ShapeDtypeStruct(shape, f32)...]
    unnamed x40 -> x42, local copies, waits for them, and re-layouts: 9.36 us -> 9.35 us
  transfers between devices with their start and end apart: 6 -> 5, of which waited for: 3 -> 2; matrix products, arithmetic and copies ran while one was open for 1% -> 1% of each run, Pallas kernels for 6% -> 10%
where the time goes in v1:
time: 128 us
  Pallas kernels  65.8 us (51%)
  waiting for transfers between devices  20.1 us (16%)
  blocking collectives  15.3 us (12%)
  local copies, waits for them, and re-layouts  11.2 us (9%)
  other arithmetic  9.82 us (8%)
  starting transfers between devices  4.13 us (3%)
  between operations  1.61 us (1%)
    pallas_call x1, Pallas kernels, reduce_all(): pl.pallas_call(reduce_kernel, out_shape=[jax.ShapeDtypeStruct(shape, f32)...  39.2 us
    ppermute x3, waiting for transfers between devices, scan_pairs(): piece = lax.ppermute(jnp.where(other > pair, up, down), 'ctx', moves)  20.1 us
    unnamed x1, blocking collectives  15.3 us
    pallas_call x1, Pallas kernels, body(): call(intra_kernel, [((wide, length), f32), ((wide, length), f32), ((heads...  13.3 us
    unnamed x42, local copies, waits for them, and re-layouts  9.35 us
    pallas_call x1, Pallas kernels, body(): call(finish_kernel, [((length, wide), bf16), ((length, wide), f32), ((hea...  7.94 us
    pallas_call x1, Pallas kernels, body(): call(prep_kernel, [((4, wide, state), f32), ((heads, 8, length), f32), ((...  5.32 us
    ppermute x3, starting transfers between devices, scan_pairs(): piece = lax.ppermute(jnp.where(other > pair, up, down), 'ctx', moves)  3.6 us
  transfers between devices with their start and end apart: 5, of which 2 were waited for; matrix products, arithmetic and copies ran while one was open for 1% of the time, Pallas kernels for 10%

profile of v1, /device:TPU:0, one launch (start us, length us, event | category | flops | bytes accessed | tf_op | source)
XLA Modules:
  0.0 127.9 jit_solution(7115189513229099545)
XLA Ops:
  0.6 0.7 copy.50.dlog_ref
  1.4 0.7 copy.49.bias_ref
  2.1 0.7 copy.46.table_ref
  2.8 1.0 copy-done
  3.8 1.0 copy-done.4
  4.9 1.0 copy-done.5
  5.9 0.7 copy-done.6
  6.7 0.7 copy-done.8
  7.3 5.3 %shard_map.145 = (f32[4,1024,128]{2,1,0:T(8,128)}, f32[16,8,256]{2,1,0:T(8,128)S(1)}, f32[4,256,128]{2,1,0:T(8,128)S(1)}, bf16[1024,256]{1,0:T(8,128)(2,1)S(1)},...) custom-call(s32[1,256]{1,0:T(1,128)S(1)} %bitcast.45, bf16[256,1024]{1,0:T(8,128)(2,1)S(1)} %copy-done.4, ...), custom_call_target="tpu_custom_call" | custom-call | tf_op jit(solution)/shard_map/pallas_call | solution.py:426
  12.7 1.7 %select_bitcast_fusion = f32[4,512,128]{2,1,0:T(8,128)S(1)} fusion(f32[4,2,512,128]{3,2,1,0:T(8,128)} %bitcast.47, pred[]{:T(512)S(6)} %eq.5), kind=kLoop, calls=%fused_computation.7 | loop fusion | flops 262144 | bytes 3145729 | tf_op jit(solution)/shard_map/jit(_where)/select_n | solution.py:386
  14.3 0.5 collective-permute-start
  14.9 0.2 fusion.3
  15.1 0.6 dynamic-slice.2
  16.4 0.1 multiply_dynamic-update-slice_fusion
  16.5 15.3 %all-reduce = f32[128]{0:T(128)S(1)} all-reduce(f32[128]{0:T(128)S(1)} %multiply_dynamic-update-slice_fusion), channel_id=2, replica_groups=mesh['ctx'=8,'head'=4] {'ctx'}, use_global_device_ids=true, to_apply=%add | all-reduce | flops 128 | bytes 1024
  31.8 0.1 reshape.116
  31.9 0.1 broadcast_in_dim.46
  32.0 0.1 exp.17
  32.2 0.0 collective-permute-done
  32.2 2.0 %bitcast_select_fusion.1 = (f32[4,512,128]{2,1,0:T(8,128)S(1)}, f32[4,512,128]{2,1,0:T(8,128)S(1)}) fusion(f32[4,512,128]{2,1,0:T(8,128)} %collective-permute-done, pred[]{:T(512)S(6)} %eq.5, f32[4,2,512,128]{3,2,1,0:T(8,128)} %bitcast.48), kind=kLoop, calls=%fused_computation.6 | loop fusion | flops 786432 | bytes 5243904 | tf_op jit(solution)/shard_map/jit(_where)/select_n | solution.py:387
  34.3 0.2 broadcast_select_fusion.4
  34.5 0.1 collective-permute-start.1
  34.6 0.1 broadcast_select_fusion.3
  34.6 0.6 collective-permute-start.2
  35.2 3.0 %collective-permute-start.3 = (f32[2,512,128]{2,1,0:T(8,128)S(1)}, f32[2,512,128]{2,1,0:T(8,128)S(1)}, u32[]{:S(2)}, u32[]{:S(2)}) collective-permute-start(f32[2,512,128]{2,1,0:T(8,128)S(1)} %get-tuple-element.81), channel_id=1, source_target_pairs={{0,24},{4,28},{8,16},{12,20},{16,8},{20,12},{24,0},{28,4},{1,25},{... | collective-permute-start | bytes 1572872 | tf_op jit(solution)/shard_map/ppermute | solution.py:400
  38.2 0.1 fusion.4
  38.3 11.1 %collective-permute-done.1 = f32[2,512,128]{2,1,0:T(8,128)S(1)} collective-permute-done((f32[2,512,128]{2,1,0:T(8,128)S(1)}, f32[2,512,128]{2,1,0:T(8,128)S(1)}, u32[]{:S(2)}, u32[]{:S(2)}) %collective-permute-start.1) | collective-permute-done | bytes 524320 | tf_op jit(solution)/shard_map/ppermute | solution.py:400
  49.4 9.0 %collective-permute-done.2 = f32[2,512,128]{2,1,0:T(8,128)S(1)} collective-permute-done((f32[2,512,128]{2,1,0:T(8,128)S(1)}, f32[2,512,128]{2,1,0:T(8,128)S(1)}, u32[]{:S(2)}, u32[]{:S(2)}) %collective-permute-start.2) | collective-permute-done | bytes 524320 | tf_op jit(solution)/shard_map/ppermute | solution.py:400
  58.4 0.0 collective-permute-done.3
  58.4 0.8 multiply_add_fusion
  59.2 0.0 copy-start.12
  59.2 0.0 copy-start.16
  59.2 1.3 %fusion.1 = f32[4,512,128]{2,1,0:T(8,128)} fusion(f32[2,512,128]{2,1,0:T(8,128)S(1)} %get-tuple-element.79, f32[2,512,128]{2,1,0:T(8,128)S(1)} %get-tuple-element.69, f32[2,512,128]{2,1,0:T(8,128)S(1)} %get-tuple-element.78, f32[2,512,128]{2,1,0:T(8,128)S(1)} %get-tuple-element.70, pred[]{:T(512)S(6)} %eq.5), kind=kLoop, calls=%fused_computation.9 | loop fusion | flops 786432 | bytes 3145729 | tf_op jit(solution)/shard_map/jit(_where)/select_n | solution.py:408
  60.5 0.0 collective-permute-start.4
  60.5 0.1 copy.51.gain_ref
  60.6 13.3 %shard_map.146 = (f32[1024,256]{1,0:T(8,128)S(1)}, f32[1024,256]{1,0:T(8,128)}, f32[16,8,256]{2,1,0:T(8,128)S(1)}, f32[4,256,128]{2,1,0:T(8,128)S(1)}) custom-call(f32[16,8,256]{2,1,0:T(8,128)S(1)} %get-tuple-element.23.rows_ref, f32[4,256,128]{2,1,0:T(8,128)S(1)} %get-tuple-element.24.bc_ref, bf16[1024,256]{1,0:T(8,128)(2,1)S(1)} %get-tuple-element.25.xt_ref, ...), custom_call_target="tpu_custom_call" | custom-call | flops 1207959552 | bytes 3145728 | tf_op jit(solution)/shard_map/pallas_call | solution.py:446
  73.9 0.0 collective-permute-done.4
  73.9 1.8 %broadcast_select_fusion.1 = (f32[4,512,128]{2,1,0:T(8,128)S(1)}, f32[4,512,128]{2,1,0:T(8,128)S(1)}) fusion(f32[4,512,128]{2,1,0:T(8,128)} %collective-permute-done.4, pred[]{:T(512)S(6)} %eq.5, f32[2,512,128]{2,1,0:T(8,128)S(1)} %copy-done.13, f32[2,512,128]{2,1,0:T(8,128)S(1)} %get-tuple-element.69, f32[2,512,128]{2,1,0:T(8,128)S(1)} %copy-done.11, ...), kind=kLoop, calls=%fused_computation.18 | loop fusion | flops 1310720 | bytes 5242881 | tf_op jit(solution)/shard_map/jit(_where)/select_n | solution.py:410
  75.8 0.0 copy-start.1
  75.8 0.0 copy-start.7
  75.8 0.0 copy-start.9
  75.8 1.5 %pad_maximum_fusion.in_ref = f32[4,1024,128]{2,1,0:T(8,128)} fusion(f32[4,512,128]{2,1,0:T(8,128)S(1)} %get-tuple-element.75, f32[4,512,128]{2,1,0:T(8,128)S(1)} %get-tuple-element.74), kind=kLoop, calls=%fused_computation | loop fusion | flops 524288 | bytes 4194304 | tf_op jit(solution)/shard_map/concatenate | solution.py:409
  77.3 7.9 %shard_map.147 = (bf16[256,1024]{1,0:T(8,128)(2,1)}, f32[256,1024]{1,0:T(8,128)}, f32[16,256]{1,0:T(8,128)}, f32[2304,128]{1,0:T(8,128)}) custom-call(s32[1,256]{1,0:T(1,128)S(1)} %bitcast.46, f32[16,256]{1,0:T(8,128)S(1)} %copy-done.7, f32[16,1]{1,0:T(8,128)S(1)} %copy.49.bias_ref, f32[16,1]{1,0:T(8,128)S(1)} %copy.50.dlog_ref, f32[16,1]{1,0:T(8,128)S(1)} %copy.51.gain_ref, ...), custom_call_target="tpu_custom_call" | custom-call | tf_op jit(solution)/shard_map/pallas_call | solution.py:466
  85.2 1.3 copy-done.2
  86.5 39.2 %shard_map.148 = (f32[2,1024,128]{2,1,0:T(8,128)S(1)}, f32[2,5,128]{2,1,0:T(8,128)S(1)}, f32[16,128]{1,0:T(8,128)S(1)}) custom-call(f32[2304,128]{1,0:T(8,128)S(1)} %copy-done.2), custom_call_target="tpu_custom_call" | custom-call | tf_op jit(solution)/shard_map/pallas_call | solution.py:328
  125.7 0.6 copy.52
  126.3 0.7 copy.53
  126.9 1.0 copy.62
  (37 shorter events, 0.1 us)
Async XLA Ops:
  2.8 1.0 copy-start
  3.8 1.0 copy-start.4
  4.9 1.0 copy-start.5
  5.9 0.7 copy-start.6
  6.6 0.7 copy-start.8
  12.6 2.2 %copy-start.14 = (f32[16]{0:T(128)S(1)}, f32[16]{0:T(128)}, u32[]{:S(2)}) copy-start(f32[16]{0:T(128)} %param.13) | copy-start | bytes 196
  12.7 2.5 %copy-start.17 = (u32[32]{0:T(128)S(1)}, u32[32]{0:T(128)}, u32[]{:S(2)}) copy-start(u32[32]{0:T(128)} %constant.55) | copy-start | bytes 388
  12.7 3.7 %copy-start.15 = (f32[16]{0:T(128)S(1)}, f32[16]{0:T(128)}, u32[]{:S(2)}) copy-start(f32[16]{0:T(128)} %param.14) | copy-start | bytes 196
  14.3 17.9 %collective-permute-start = (f32[4,512,128]{2,1,0:T(8,128)S(1)}, f32[4,512,128]{2,1,0:T(8,128)}, u32[]{:S(2)}, u32[]{:S(2)}) collective-permute-start(f32[4,512,128]{2,1,0:T(8,128)S(1)} %select_bitcast_fusion), channel_id=1, source_target_pairs={{0,4},{4,0},{8,12},{12,8},{16,20},{20,16},{24,28},{28,24},{1,5},{5... | collective-permute-start | bytes 3145736 | tf_op jit(solution)/shard_map/ppermute | solution.py:386
  34.5 14.9 %collective-permute-start.1 = (f32[2,512,128]{2,1,0:T(8,128)S(1)}, f32[2,512,128]{2,1,0:T(8,128)S(1)}, u32[]{:S(2)}, u32[]{:S(2)}) collective-permute-start(f32[2,512,128]{2,1,0:T(8,128)S(1)} %get-tuple-element.71), channel_id=1, source_target_pairs={{0,8},{4,12},{8,0},{12,4},{16,24},{20,28},{24,16},{28,20},{1,9},{5... | collective-permute-start | bytes 1572872 | tf_op jit(solution)/shard_map/ppermute | solution.py:400
  34.6 23.7 %collective-permute-start.2 = (f32[2,512,128]{2,1,0:T(8,128)S(1)}, f32[2,512,128]{2,1,0:T(8,128)S(1)}, u32[]{:S(2)}, u32[]{:S(2)}) collective-permute-start(f32[2,512,128]{2,1,0:T(8,128)S(1)} %get-tuple-element.80), channel_id=1, source_target_pairs={{0,16},{4,20},{8,24},{12,28},{16,0},{20,4},{24,8},{28,12},{1,17},{... | collective-permute-start | bytes 1572872 | tf_op jit(solution)/shard_map/ppermute | solution.py:400
  35.2 23.2 %collective-permute-start.3 = (f32[2,512,128]{2,1,0:T(8,128)S(1)}, f32[2,512,128]{2,1,0:T(8,128)S(1)}, u32[]{:S(2)}, u32[]{:S(2)}) collective-permute-start(f32[2,512,128]{2,1,0:T(8,128)S(1)} %get-tuple-element.81), channel_id=1, source_target_pairs={{0,24},{4,28},{8,16},{12,20},{16,8},{20,12},{24,0},{28,4},{1,25},{... | collective-permute-start | bytes 1572872 | tf_op jit(solution)/shard_map/ppermute | solution.py:400
  59.2 1.3 %copy-start.10 = (f32[2,512,128]{2,1,0:T(8,128)}, f32[2,512,128]{2,1,0:T(8,128)S(1)}, u32[]{:S(2)}) copy-start(f32[2,512,128]{2,1,0:T(8,128)S(1)} %get-tuple-element.78) | copy-start | bytes 1572868
  59.2 1.3 %copy-start.12 = (f32[2,512,128]{2,1,0:T(8,128)}, f32[2,512,128]{2,1,0:T(8,128)S(1)}, u32[]{:S(2)}) copy-start(f32[2,512,128]{2,1,0:T(8,128)S(1)} %get-tuple-element.79) | copy-start | bytes 1572868
  59.2 1.3 %copy-start.16 = (f32[16]{0:T(128)S(1)}, f32[16]{0:T(128)}, u32[]{:S(2)}) copy-start(f32[16]{0:T(128)} %param.15) | copy-start | bytes 196
  60.5 13.4 %collective-permute-start.4 = (f32[4,512,128]{2,1,0:T(8,128)}, f32[4,512,128]{2,1,0:T(8,128)}, u32[]{:S(2)}, u32[]{:S(2)}) collective-permute-start(f32[4,512,128]{2,1,0:T(8,128)} %fusion.1), channel_id=1, source_target_pairs={{0,4},{4,0},{8,12},{12,8},{16,20},{20,16},{24,28},{28,24},{1,5},{5... | collective-permute-start | bytes 3145736 | tf_op jit(solution)/shard_map/ppermute | solution.py:408
  60.6 13.3 %copy-start.11 = (f32[2,512,128]{2,1,0:T(8,128)S(1)}, f32[2,512,128]{2,1,0:T(8,128)}, u32[]{:S(2)}) copy-start(f32[2,512,128]{2,1,0:T(8,128)} %copy-done.10) | copy-start | bytes 1572868
  60.6 13.3 %copy-start.13 = (f32[2,512,128]{2,1,0:T(8,128)S(1)}, f32[2,512,128]{2,1,0:T(8,128)}, u32[]{:S(2)}) copy-start(f32[2,512,128]{2,1,0:T(8,128)} %copy-done.12) | copy-start | bytes 1572868
  73.9 1.9 %copy-start.3 = (f32[1024,256]{1,0:T(8,128)}, f32[1024,256]{1,0:T(8,128)S(1)}, u32[]{:S(2)}) copy-start(f32[1024,256]{1,0:T(8,128)S(1)} %get-tuple-element.29.y_ref) | copy-start | bytes 3145732
  75.8 1.5 %copy-start.1 = (bf16[256,1024]{1,0:T(8,128)(2,1)S(1)}, bf16[256,1024]{1,0:T(8,128)(2,1)}, u32[]{:S(2)}) copy-start(bf16[256,1024]{1,0:T(8,128)(2,1)} %feat_ref.3) | copy-start | bytes 1572868
  75.8 1.5 %copy-start.7 = (f32[16,256]{1,0:T(8,128)S(1)}, f32[16,256]{1,0:T(8,128)}, u32[]{:S(2)}) copy-start(f32[16,256]{1,0:T(8,128)} %step_ref.3) | copy-start | bytes 49156
  75.8 1.5 %copy-start.9 = (s32[256]{0:T(256)S(1)}, s32[256]{0:T(256)}, u32[]{:S(2)}) copy-start(s32[256]{0:T(256)} %param.10) | copy-start | bytes 3076
  85.2 1.3 copy-start.2

commit v2 on v1

--- a/solution.py
+++ b/solution.py
@@ -62,7 +62,7 @@
 
 def prep_kernel(
     tok_ref, x_ref, u_ref, step_ref, bias_ref, dlog_ref, table_ref, feat_ref, proj_ref,
-    states_ref, rows_ref, bc_ref, xt_ref, ut_ref, flip_ref, tab, wide_hi, wide_lo,
+    states_ref, rows_ref, bc_ref, xt_ref, ut_ref, flip_ref, dec_ref, tab, wide_hi, wide_lo,
 ):
     heads, length = step_ref.shape
     width = x_ref.shape[1] // heads
@@ -72,6 +72,7 @@
     cum = times_exact(rate, (row <= col).astype(bf16), NN)
     total = cum[:, length - 1 : length]
     excl = cum - rate
+    dec_ref[...] = jnp.broadcast_to(jnp.exp(total), dec_ref.shape)
     ef, wf = jnp.exp(cum), jnp.exp(total - cum) * delta
     er, wr = jnp.exp(total - excl), jnp.exp(excl) * delta
     for k, value in enumerate((cum, excl, delta, ef, wf, er, wr, rate)):
@@ -113,8 +114,126 @@
         states_ref[k] = mm3((wide_hi[...], wide_lo[...]), split(right), NN)
 
 
+def exchange_peers():
+    ctx, head = lax.axis_index("ctx"), lax.axis_index("head")
+    core, pair = ctx % 2, ctx // 2
+    x, y = pair % 2, pair // 2
+    moves = (1 - 2 * x, 2 - 4 * y, 3 - 2 * x - 4 * y)
+    higher = (1 - x, 1 - y, 1 - y)
+    return ctx, head, core, pair, moves, higher
+
+
+def exchange_copies(states_ref, dec_ref, decs, own, got, totals, pieces, inc, send, recv, local):
+    ctx, head, core, pair, moves, higher = exchange_peers()
+    half = own.shape[1]
+    partner = ctx + 1 - 2 * core
+    keep = pl.ds(pl.multiple_of(core * half, 8), half)
+    give = pl.ds(pl.multiple_of((1 - core) * half, 8), half)
+    load = lambda: pltpu.make_async_copy(states_ref.at[:, keep], own, local)
+    swap = lambda: remote(states_ref.at[:, give], got, send.at[0], recv.at[0], partner, head)
+    chips = lambda: [
+        remote(
+            totals.at[pl.ds(2 * (1 - up), 2)], pieces.at[k], send.at[1 + k], recv.at[1 + k],
+            ctx + 2 * move, head,
+        )
+        for k, (move, up) in enumerate(zip(moves, higher))
+    ]
+    back = lambda: remote(totals, inc.at[:, keep], send.at[4], recv.at[4], partner, head)
+    rates = lambda: [
+        remote(
+            decs.at[ctx], decs.at[ctx], send.at[4 + d], recv.at[4 + d],
+            lax.rem(ctx + d, 8), head,
+        )
+        for d in range(1, 8)
+    ]
+    return load, swap, chips, back, rates
+
+
+def exchange(states_ref, dec_ref, out_ref, decs, own, got, totals, pieces, inc, send, recv, local):
+    refs = (states_ref, dec_ref, decs, own, got, totals, pieces, inc, send, recv, local)
+    ctx, head, core, pair, moves, higher = exchange_peers()
+    step, last = pl.program_id(0), pl.num_programs(0) - 1
+    heads = dec_ref.shape[0] // 2
+    width = own.shape[1] // heads
+    first = core == 0
+
+    def decay(device, h):
+        return decs[device, pl.ds(core * heads + h, 1), :]
+
+    @pl.when(step == 0)
+    def _():
+        load, swap, _, _, rates = exchange_copies(*refs)
+        greet([(lax.rem(ctx + d, 8), head) for d in range(1, 8)])
+        load().start()
+        swap().start()
+        decs[ctx] = dec_ref[...]
+        for copy in rates():
+            copy.start()
+
+    @pl.when(step == 3)
+    def _():
+        load, swap, chips, _, rates = exchange_copies(*refs)
+        load().wait()
+        for copy in [swap()] + rates():
+            copy.wait()
+        for h in range(heads):
+            at = slice(h * width, (h + 1) * width)
+            low, high = decay(2 * pair, h), decay(2 * pair + 1, h)
+            totals[0:2, at, :] = own[0:2, at, :] * jnp.where(first, high, 1.0) + got[
+                0:2, at, :
+            ] * jnp.where(first, 1.0, high)
+            totals[2:4, at, :] = own[2:4, at, :] * jnp.where(first, 1.0, low) + got[
+                2:4, at, :
+            ] * jnp.where(first, low, 1.0)
+        for copy in chips():
+            copy.start()
+
+    @pl.when(step == last)
+    def _():
+        _, _, chips, back, _ = exchange_copies(*refs)
+        for copy in chips():
+            copy.wait()
+        keep = lambda h: pl.ds(
+            pl.multiple_of(core * heads * width + h * width, 8), width
+        )
+        one = jnp.where(first, 1.0, 0.0)
+        for h in range(heads):
+            at = slice(h * width, (h + 1) * width)
+            low, high = decay(2 * pair, h), decay(2 * pair + 1, h)
+            both = {c: decay(2 * c, h) * decay(2 * c + 1, h) for c in (1, 2)}
+            up, down = 0.0, 0.0
+            for k, (move, higher_k) in enumerate(zip(moves, higher)):
+                other = pair + move
+                factor = 1.0
+                for c in (1, 2):
+                    inside = (c - pair) * (other - c) > 0
+                    factor = factor * jnp.where(inside, both[c], 1.0)
+                piece = pieces[k, :, at, :]
+                up += piece * jnp.where(higher_k == 0, factor, 0.0)
+                down += piece * jnp.where(higher_k == 1, factor, 0.0)
+            inc[0:2, keep(h), :] = up * jnp.where(first, 1.0, low) + got[0:2, at, :] * (1.0 - one)
+            inc[2:4, keep(h), :] = down * jnp.where(first, high, 1.0) + got[2:4, at, :] * one
+            totals[0:2, at, :] = up * jnp.where(first, low, 1.0) + own[0:2, at, :] * one
+            totals[2:4, at, :] = down * jnp.where(first, 1.0, high) + own[2:4, at, :] * (1.0 - one)
+        copy = back()
+        copy.start()
+        copy.wait()
+        out_ref[...] = inc[...]
+
+
+def intra_exchange_kernel(
+    states_ref, dec_ref, rows_ref, bc_ref, xt_ref, ut_ref, y_ref, dx_ref, sums_ref, dbc_ref,
+    out_ref, aff_f, aff_r, total, *scratch,
+):
+    intra_kernel(
+        rows_ref, bc_ref, xt_ref, ut_ref, y_ref, dx_ref, sums_ref, dbc_ref, aff_f, aff_r, total,
+        exchange_step=lambda: exchange(states_ref, dec_ref, out_ref, *scratch),
+    )
+
+
 def intra_kernel(
-    rows_ref, bc_ref, xt_ref, ut_ref, y_ref, dx_ref, sums_ref, dbc_ref, aff_f, aff_r, total
+    rows_ref, bc_ref, xt_ref, ut_ref, y_ref, dx_ref, sums_ref, dbc_ref, aff_f, aff_r, total,
+    exchange_step=None,
 ):
     length = xt_ref.shape[1]
     head = pl.program_id(0)
@@ -158,6 +277,9 @@
         dbc_ref[1] = mm3(g_fwd, b_fwd, TN)
         dbc_ref[2] = mm3(g_rev, c_rev, NN)
         dbc_ref[3] = mm3(g_rev, b_rev, TN)
+
+    if exchange_step is not None:
+        exchange_step()
 
 
 def finish_kernel(
@@ -374,43 +496,6 @@
     return jnp.concatenate([up, down], axis=0)
 
 
-def scan_pairs(states, decays):
-    count, mine = lax.axis_size("ctx"), lax.axis_index("ctx")
-    core, pair = mine % 2, mine // 2
-    pairs = count // 2
-    half = states.shape[1] // 2
-    swap = [(i, i ^ 1) for i in range(count)]
-    halves = states.reshape(4, 2, half, states.shape[2])
-    first = core == 0
-    own = jnp.where(first, halves[:, 0], halves[:, 1])
-    got = lax.ppermute(jnp.where(first, halves[:, 1], halves[:, 0]), "ctx", swap)
-    low, high = jnp.where(first, own, got), jnp.where(first, got, own)
-    decays = lax.dynamic_slice_in_dim(decays, core * half, half, 1)
-    by_pair = decays.reshape(pairs, 2, half)
-    both = by_pair[:, 0] * by_pair[:, 1]
-    dec_low = lax.dynamic_index_in_dim(by_pair[:, 0], pair, 0, False)[:, None]
-    dec_high = lax.dynamic_index_in_dim(by_pair[:, 1], pair, 0, False)[:, None]
-    up = low[:2] * dec_high + high[:2]
-    down = high[2:] * dec_low + low[2:]
-    index = jnp.arange(pairs)[:, None]
-    sum_up, sum_down = 0.0, 0.0
-    for k in range(1, pairs):
-        other = pair ^ k
-        moves = [(i, i ^ (2 * k)) for i in range(count)]
-        piece = lax.ppermute(jnp.where(other > pair, up, down), "ctx", moves)
-        between = (index > jnp.minimum(pair, other)) & (index < jnp.maximum(pair, other))
-        factor = jnp.prod(jnp.where(between, both, 1.0), axis=0)[:, None]
-        sum_up += piece * jnp.where(other < pair, factor, 0.0)
-        sum_down += piece * jnp.where(other > pair, factor, 0.0)
-    for_low = jnp.concatenate([sum_up, sum_down * dec_high + high[2:]], axis=0)
-    for_high = jnp.concatenate([sum_up * dec_low + low[:2], sum_down], axis=0)
-    keep = jnp.where(first, for_low, for_high)
-    other_half = lax.ppermute(jnp.where(first, for_high, for_low), "ctx", swap)
-    return jnp.concatenate(
-        [jnp.where(first, keep, other_half), jnp.where(first, other_half, keep)], axis=1
-    )
-
-
 def body(
     tokens, inputs, step_raw, step_bias, decay_log, skip_gain, bc_table, features, bc_proj, cotangent
 ):
@@ -420,10 +505,7 @@
     feat, state = bc_proj.shape[1:]
     tok = tokens.reshape(1, length)
     bias, logs, gain = (v.reshape(heads, 1) for v in (step_bias, decay_log, skip_gain))
-    totals = -jnp.exp(decay_log) * jnp.sum(jax.nn.softplus(step_raw + bias), axis=1)
-    decays = jnp.exp(jnp.repeat(lax.all_gather(totals, "ctx"), width, axis=1))
-
-    states, rows, bc, xt, ut, flipped = call(
+    states, rows, bc, xt, ut, flipped, decay = call(
         prep_kernel,
         [
             ((4, wide, state), f32),
@@ -432,35 +514,67 @@
             ((wide, length), bf16),
             ((wide, length), bf16),
             ((length, feat), bf16),
+            ((heads, state), f32),
         ],
         [((16, state), f32), ((wide, length), bf16), ((wide, length), bf16)],
     )(tok, inputs, cotangent, step_raw, bias, logs, bc_table, features, bc_proj)
 
-    count = lax.axis_size("ctx")
-    paired = count <= 16 and count & (count - 1) == 0 and count > 2 and heads % 2 == 0
-    incoming = (scan_pairs if paired else scan_gather)(states, decays)
-
     per_head = pl.BlockSpec((width, length), lambda h: (h, 0))
     per_rows = pl.BlockSpec((1, 8, length), lambda h: (h, 0, 0))
     whole = pl.BlockSpec((4, length, state), lambda h: (0, 0, 0))
-    y, dx, sums, dbc = call(
-        intra_kernel,
-        [
-            ((wide, length), f32),
-            ((wide, length), f32),
-            ((heads, 8, length), f32),
-            ((4, length, state), f32),
-        ],
-        [((length, length), f32)] * 3,
-        pl.CostEstimate(
-            flops=heads * length * length * width * 18,
-            bytes_accessed=wide * length * 12,
-            transcendentals=heads * length * length,
-        ),
-        grid=(heads,),
-        in_specs=[per_rows, whole, per_head, per_head],
-        out_specs=[per_head, per_head, per_rows, whole],
-    )(rows, bc, xt, ut)
+    full = pl.BlockSpec((4, wide, state), lambda h: (0, 0, 0))
+    outs = [
+        ((wide, length), f32),
+        ((wide, length), f32),
+        ((heads, 8, length), f32),
+        ((4, length, state), f32),
+    ]
+    squares = [((length, length), f32)] * 3
+    in_specs, out_specs = [per_rows, whole, per_head, per_head], [per_head, per_head, per_rows, whole]
+    if lax.axis_size("ctx") == 8 and heads % 16 == 0:
+        half = wide // 2
+        y, dx, sums, dbc, incoming = pl.pallas_call(
+            intra_exchange_kernel,
+            grid=(heads,),
+            out_shape=[
+                jax.ShapeDtypeStruct(*out) for out in outs + [((4, wide, state), f32)]
+            ],
+            in_specs=[
+                pl.BlockSpec(memory_space=pl.ANY),
+                pl.BlockSpec((heads, state), lambda h: (0, 0)),
+            ]
+            + in_specs,
+            out_specs=out_specs + [full],
+            scratch_shapes=[pltpu.VMEM(*square) for square in squares]
+            + [pltpu.VMEM((8, heads, state), f32)]
+            + [pltpu.VMEM((4, half, state), f32)] * 3
+            + [
+                pltpu.VMEM((3, 2, half, state), f32),
+                pltpu.VMEM((4, wide, state), f32),
+                pltpu.SemaphoreType.DMA((12,)),
+                pltpu.SemaphoreType.DMA((12,)),
+                pltpu.SemaphoreType.DMA,
+            ],
+            compiler_params=pltpu.CompilerParams(
+                collective_id=1, has_side_effects=True, **PARAMS
+            ),
+        )(states, decay, rows, bc, xt, ut)
+    else:
+        decays = jnp.repeat(lax.all_gather(decay[:, 0], "ctx"), width, axis=1)
+        incoming = scan_gather(states, decays)
+        y, dx, sums, dbc = call(
+            intra_kernel,
+            outs,
+            squares,
+            pl.CostEstimate(
+                flops=heads * length * length * width * 18,
+                bytes_accessed=wide * length * 12,
+                transcendentals=heads * length * length,
+            ),
+            grid=(heads,),
+            in_specs=in_specs,
+            out_specs=out_specs,
+        )(rows, bc, xt, ut)
 
     sum_rows = 2 * feat + 16 + heads * lax.axis_size("head")
     mixed, input_grad, step_grad, local_sums = call(

time: 128 us -> 103 us (0.80)
  Pallas kernels: 65.8 us -> 90.4 us
  waiting for transfers between devices: 20.1 us -> 0 us
  blocking collectives: 15.3 us -> 0 us
  other arithmetic: 9.82 us -> 0 us
  starting transfers between devices: 4.13 us -> 0 us
    pallas_call x1, Pallas kernels: 13.3 us -> 37.8 us  [body(): pl.pallas_call(intra_exchange_kernel, grid=(heads,), out_shape=[jax.Shape...]
    ppermute x5 -> x0, waiting for transfers between devices: 20.1 us -> none  [the longest x3 20.1 us: scan_pairs(): piece = lax.ppermute(jnp.where(other > pair, up, down), 'ctx', moves)]
    unnamed x1 -> x0, blocking collectives: 15.3 us -> none
    select_n x8 -> x0, other arithmetic: 7.13 us -> none  [the longest x1 2.05 us: scan_pairs(): low, high = (jnp.where(first, own, got), jnp.where(first, got, own))]
    ppermute x5 -> x0, starting transfers between devices: 4.13 us -> none  [the longest x3 3.6 us: scan_pairs(): piece = lax.ppermute(jnp.where(other > pair, up, down), 'ctx', moves)]
    concatenate x1 -> x0, other arithmetic: 1.46 us -> none  [scan_pairs(): jnp.concatenate([jnp.where(first, keep, other_half), jnp.where(first, oth...]
    unnamed x42 -> x20, local copies, waits for them, and re-layouts: 9.35 us -> 9.67 us
  transfers between devices with their start and end apart: 5 -> 0, of which waited for: 2 -> 0; matrix products, arithmetic and copies ran while one was open for 1% -> 0% of each run, Pallas kernels for 10% -> 0%
where the time goes in v2:
time: 103 us
  Pallas kernels  90.4 us (88%)
  local copies, waits for them, and re-layouts  11.9 us (12%)
    pallas_call x1, Pallas kernels, reduce_all(): pl.pallas_call(reduce_kernel, out_shape=[jax.ShapeDtypeStruct(shape, f32)...  39.2 us
    pallas_call x1, Pallas kernels, body(): pl.pallas_call(intra_exchange_kernel, grid=(heads,), out_shape=[jax.Shape...  37.8 us
    unnamed x20, local copies, waits for them, and re-layouts  9.67 us
    pallas_call x1, Pallas kernels, body(): call(finish_kernel, [((length, wide), bf16), ((length, wide), f32), ((hea...  8.11 us
    pallas_call x1, Pallas kernels, body(): call(prep_kernel, [((4, wide, state), f32), ((heads, 8, length), f32), ((...  5.36 us
    reshape x3, local copies, waits for them, and re-layouts, body(): v.reshape(heads, 1)  2.19 us

profile of v2, /device:TPU:0, one launch (start us, length us, event | category | flops | bytes accessed | tf_op | source)
XLA Modules:
  0.0 103.0 jit_solution(11513173176733847188)
XLA Ops:
  0.6 0.7 copy.19.bias_ref
  1.4 0.7 copy.20.dlog_ref
  2.1 0.7 copy.21.gain_ref
  2.8 0.7 copy.18.table_ref
  3.5 0.0 copy-start
  3.5 1.0 %copy-done = bf16[256,1024]{1,0:T(8,128)(2,1)S(1)} copy-done((bf16[256,1024]{1,0:T(8,128)(2,1)S(1)}, bf16[256,1024]{1,0:T(8,128)(2,1)}, u32[]{:S(2)}) %copy-start) | copy-done | bytes 524312
  4.6 0.0 copy-start.4
  4.6 1.0 %copy-done.4 = bf16[256,1024]{1,0:T(8,128)(2,1)S(1)} copy-done((bf16[256,1024]{1,0:T(8,128)(2,1)S(1)}, bf16[256,1024]{1,0:T(8,128)(2,1)}, u32[]{:S(2)}) %copy-start.4) | copy-done | bytes 524312
  5.6 0.0 copy-start.5
  5.6 1.0 %copy-done.5 = bf16[256,1024]{1,0:T(8,128)(2,1)S(1)} copy-done((bf16[256,1024]{1,0:T(8,128)(2,1)S(1)}, bf16[256,1024]{1,0:T(8,128)(2,1)}, u32[]{:S(2)}) %copy-start.5) | copy-done | bytes 524312
  6.6 0.0 copy-start.6
  6.6 0.7 copy-done.6
  7.4 0.0 copy-start.7
  7.4 0.7 copy-done.7
  8.0 5.4 %shard_map.145 = (f32[4,1024,128]{2,1,0:T(8,128)}, f32[16,8,256]{2,1,0:T(8,128)S(1)}, f32[4,256,128]{2,1,0:T(8,128)S(1)}, bf16[1024,256]{1,0:T(8,128)(2,1)S(1)},...) custom-call(s32[1,256]{1,0:T(1,128)S(1)} %bitcast.6, ...), custom_call_target="tpu_custom_call" | custom-call | tf_op jit(solution)/shard_map/pallas_call | solution.py:508
  13.4 0.0 copy-start.1
  13.4 37.8 %shard_map.146 = (f32[1024,256]{1,0:T(8,128)S(1)}, f32[1024,256]{1,0:T(8,128)}, f32[16,8,256]{2,1,0:T(8,128)S(1)}, f32[4,256,128]{2,1,0:T(8,128)S(1)}, f32[4,1024,128]{2,1,0:T(8,128)}) custom-call(f32[4,1024,128]{2,1,0:T(8,128)} %get-tuple-element.26.states_ref, f32[16,128]{1,0:T(8,128)S(1)} %get-tuple-element.27.dec_ref, ...), custom_call_target="tpu_custom_call" | custom-call | tf_op jit(solution)/shard_map/pallas_call | solution.py:536
  51.2 0.0 copy-start.3
  51.2 1.0 copy-done.3
  52.2 0.0 copy-done.1
  52.2 8.1 %shard_map.147 = (bf16[256,1024]{1,0:T(8,128)(2,1)}, f32[256,1024]{1,0:T(8,128)}, f32[16,256]{1,0:T(8,128)}, f32[2304,128]{1,0:T(8,128)}) custom-call(s32[1,256]{1,0:T(1,128)S(1)} %bitcast.7, f32[16,256]{1,0:T(8,128)S(1)} %copy-done.6, f32[16,1]{1,0:T(8,128)S(1)} %copy.19.bias_ref, f32[16,1]{1,0:T(8,128)S(1)} %copy.20.dlog_ref, f32[16,1]{1,0:T(8,128)S(1)} %copy.21.gain_ref, ...), custom_call_target="tpu_custom_call" | custom-call | tf_op jit(solution)/shard_map/pallas_call | solution.py:580
  60.3 0.0 copy-start.2
  60.3 1.3 %copy-done.2 = f32[2304,128]{1,0:T(8,128)S(1)} copy-done((f32[2304,128]{1,0:T(8,128)S(1)}, f32[2304,128]{1,0:T(8,128)}, u32[]{:S(2)}) %copy-start.2) | copy-done | bytes 1179672
  61.5 39.2 %shard_map.148 = (f32[2,1024,128]{2,1,0:T(8,128)S(1)}, f32[2,5,128]{2,1,0:T(8,128)S(1)}, f32[16,128]{1,0:T(8,128)S(1)}) custom-call(f32[2304,128]{1,0:T(8,128)S(1)} %copy-done.2), custom_call_target="tpu_custom_call" | custom-call | tf_op jit(solution)/shard_map/pallas_call | solution.py:450
  100.8 0.6 copy.22
  101.4 0.7 copy.23
  102.0 1.0 copy.25
  (1 shorter events, 0.0 us)
Async XLA Ops:
  3.5 1.0 %copy-start = (bf16[256,1024]{1,0:T(8,128)(2,1)S(1)}, bf16[256,1024]{1,0:T(8,128)(2,1)}, u32[]{:S(2)}) copy-start(bf16[256,1024]{1,0:T(8,128)(2,1)} %feat_ref.3) | copy-start | bytes 1572868
  4.6 1.0 %copy-start.4 = (bf16[256,1024]{1,0:T(8,128)(2,1)S(1)}, bf16[256,1024]{1,0:T(8,128)(2,1)}, u32[]{:S(2)}) copy-start(bf16[256,1024]{1,0:T(8,128)(2,1)} %x_ref.1) | copy-start | bytes 1572868
  5.6 1.0 %copy-start.5 = (bf16[256,1024]{1,0:T(8,128)(2,1)S(1)}, bf16[256,1024]{1,0:T(8,128)(2,1)}, u32[]{:S(2)}) copy-start(bf16[256,1024]{1,0:T(8,128)(2,1)} %u_ref.1) | copy-start | bytes 1572868
  6.6 0.7 copy-start.6
  7.4 0.7 copy-start.7
  13.4 38.8 %copy-start.1 = (bf16[256,1024]{1,0:T(8,128)(2,1)S(1)}, bf16[256,1024]{1,0:T(8,128)(2,1)}, u32[]{:S(2)}) copy-start(bf16[256,1024]{1,0:T(8,128)(2,1)} %feat_ref.3) | copy-start | bytes 1572868
  51.2 1.0 copy-start.3
  60.3 1.3 %copy-start.2 = (f32[2304,128]{1,0:T(8,128)S(1)}, f32[2304,128]{1,0:T(8,128)}, u32[]{:S(2)}) copy-start(f32[2304,128]{1,0:T(8,128)} %get-tuple-element.40.part_ref) | copy-start | bytes 3538948

commit v3 on v2

--- a/solution.py
+++ b/solution.py
@@ -397,45 +397,72 @@
     partners = [ctx + (1 - 2 * bit) * stride for bit, stride in zip(bits, (1, 2, 4))]
     others = [lax.rem(head + d, 4) for d in (1, 2, 3)]
     greet([(p, head) for p in partners] + [(ctx, o) for o in others])
-    start, size = 0, part_ref.shape[0]
+    def run(copies):
+        for copy in copies:
+            copy.start()
+        for copy in copies:
+            copy.wait()
+
+    def span(start, size):
+        return pl.ds(pl.multiple_of(start, 8), size)
+
+    size = part_ref.shape[0] // 2
+    base = bits[0] * size
+    core_keep = span(base, size)
+    core_give = span((1 - bits[0]) * size, size)
+    run([remote(part_ref.at[core_give], got1, send.at[0], recv.at[0], partners[0], head)])
+    acc[core_keep, :] = part_ref[core_keep, :] + got1[...]
+    size //= 2
+    starts = [base, base + size]
+    orders = ((1, 2), (2, 1))
     kept = []
-    for i, (bit, partner, got) in enumerate(zip(bits, partners, (got1, got2, got3))):
+    for i, got in enumerate((got2, got3)):
         size //= 2
-        keep = pl.ds(pl.multiple_of(start + bit * size, 8), size)
-        give = pl.ds(pl.multiple_of(start + (1 - bit) * size, 8), size)
-        source = part_ref if i == 0 else acc
-        copy = remote(source.at[give], got, send.at[i], recv.at[i], partner, head)
-        copy.start()
-        copy.wait()
-        acc[keep, :] = source[keep, :] + got[...]
-        kept.append(keep)
-        start = start + bit * size
+        axes = [order[i] for order in orders]
+        keeps = [span(at + bits[axis] * size, size) for at, axis in zip(starts, axes)]
+        gives = [span(at + (1 - bits[axis]) * size, size) for at, axis in zip(starts, axes)]
+        slots = [1 + 2 * i + s for s in range(2)]
+        run(
+            [
+                remote(acc.at[gives[s]], got.at[s], send.at[slots[s]], recv.at[slots[s]],
+                       partners[axes[s]], head)
+                for s in range(2)
+            ]
+        )
+        for s in range(2):
+            acc[keeps[s], :] = acc[keeps[s], :] + got[s]
+        kept.append((keeps, axes))
+        starts = [at + bits[axis] * size for at, axis in zip(starts, axes)]
     size //= 4
-    quarter = lambda z: pl.ds(pl.multiple_of(start + z * size, 8), size)
-    copies = [
-        remote(acc.at[quarter(o)], gotz.at[d], sendz.at[d], recvz.at[d], ctx, o)
-        for d, o in enumerate(others)
-    ]
-    for copy in copies:
-        copy.start()
-    for copy in copies:
-        copy.wait()
-    mine = quarter(head)
-    out[mine, :] = acc[mine, :] + gotz[0] + gotz[1] + gotz[2]
-    copies = [
-        remote(out.at[mine], out.at[mine], sendz.at[3 + d], recvz.at[3 + d], ctx, o)
-        for d, o in enumerate(others)
-    ]
-    for copy in copies:
-        copy.start()
-    for copy in copies:
-        copy.wait()
-    for i in (2, 1, 0):
-        copy = remote(
-            out.at[kept[i]], out.at[kept[i]], send.at[3 + i], recv.at[3 + i], partners[i], head
+    both = [(s, d, o) for s in range(2) for d, o in enumerate(others)]
+    run(
+        [
+            remote(acc.at[span(starts[s] + o * size, size)], gotz.at[s, d],
+                   sendz.at[3 * s + d], recvz.at[3 * s + d], ctx, o)
+            for s, d, o in both
+        ]
+    )
+    mine = [span(at + head * size, size) for at in starts]
+    for s in range(2):
+        out[mine[s], :] = acc[mine[s], :] + gotz[s, 0] + gotz[s, 1] + gotz[s, 2]
+    run(
+        [
+            remote(out.at[mine[s]], out.at[mine[s]],
+                   sendz.at[6 + 3 * s + d], recvz.at[6 + 3 * s + d], ctx, o)
+            for s, d, o in both
+        ]
+    )
+    for i in (1, 0):
+        keeps, axes = kept[i]
+        slots = [5 + 2 * i + s for s in range(2)]
+        run(
+            [
+                remote(out.at[keeps[s]], out.at[keeps[s]], send.at[slots[s]], recv.at[slots[s]],
+                       partners[axes[s]], head)
+                for s in range(2)
+            ]
         )
-        copy.start()
-        copy.wait()
+    run([remote(out.at[core_keep], out.at[core_keep], send.at[9], recv.at[9], partners[0], head)])
     feat, heads = proj_ref.shape[1], heads_ref.shape[0]
     for k in range(2):
         proj_ref[k] = out[k * feat : (k + 1) * feat, :]
@@ -451,10 +478,11 @@
             reduce_kernel,
             out_shape=[jax.ShapeDtypeStruct(shape, f32) for shape in shapes],
             scratch_shapes=[
-                pltpu.VMEM((rows // cut, state), f32) for cut in (1, 1, 2, 4, 8)
+                pltpu.VMEM((rows // cut, state), f32) for cut in (1, 1, 2)
             ]
-            + [pltpu.VMEM((3, rows // 32, state), f32)]
-            + [pltpu.SemaphoreType.DMA((6,))] * 4,
+            + [pltpu.VMEM((2, rows // cut, state), f32) for cut in (8, 16)]
+            + [pltpu.VMEM((2, 3, rows // 64, state), f32)]
+            + [pltpu.SemaphoreType.DMA((12,))] * 4,
             in_specs=[pl.BlockSpec(memory_space=pltpu.VMEM)],
             compiler_params=pltpu.CompilerParams(
                 collective_id=0, has_side_effects=True, **PARAMS
@@ -583,7 +611,7 @@
             ((length, wide), bf16),
             ((length, wide), f32),
             ((heads, length), f32),
-            ((pl.cdiv(sum_rows, 256) * 256, state), f32),
+            ((pl.cdiv(sum_rows, 512) * 512, state), f32),
         ],
         [
             ((4, wide, length), f32),

time: 103 us -> 99 us (0.961)
  Pallas kernels: 90.4 us -> 85.9 us
    pallas_call x1, Pallas kernels: 39.2 us -> 34.6 us  [reduce_all(): pl.pallas_call(reduce_kernel, out_shape=[jax.ShapeDtypeStruct(shape, f32)...]
where the time goes in v3:
time: 99 us; the launch traced here: 98.5 us
  Pallas kernels  85.9 us (87%)
  local copies, waits for them, and re-layouts  11.9 us (12%)
    pallas_call x1, Pallas kernels, body(): pl.pallas_call(intra_exchange_kernel, grid=(heads,), out_shape=[jax.Shape...  37.8 us
    pallas_call x1, Pallas kernels, reduce_all(): pl.pallas_call(reduce_kernel, out_shape=[jax.ShapeDtypeStruct(shape, f32)...  34.6 us
    unnamed x20, local copies, waits for them, and re-layouts  9.71 us
    pallas_call x1, Pallas kernels, body(): call(finish_kernel, [((length, wide), bf16), ((length, wide), f32), ((hea...  8.18 us
    pallas_call x1, Pallas kernels, body(): call(prep_kernel, [((4, wide, state), f32), ((heads, 8, length), f32), ((...  5.36 us
    reshape x3, local copies, waits for them, and re-layouts, body(): v.reshape(heads, 1)  2.19 us

profile of v3, /device:TPU:0, one launch (start us, length us, event | category | flops | bytes accessed | tf_op | source)
XLA Modules:
  0.0 98.5 jit_solution(8360486594199987908)
XLA Ops:
  0.6 0.7 copy.19.bias_ref
  1.4 0.7 copy.20.dlog_ref
  2.1 0.7 copy.21.gain_ref
  2.8 0.7 copy.18.table_ref
  3.5 0.0 copy-start
  3.5 1.0 %copy-done = bf16[256,1024]{1,0:T(8,128)(2,1)S(1)} copy-done((bf16[256,1024]{1,0:T(8,128)(2,1)S(1)}, bf16[256,1024]{1,0:T(8,128)(2,1)}, u32[]{:S(2)}) %copy-start) | copy-done | bytes 524312
  4.6 0.0 copy-start.4
  4.6 1.0 %copy-done.4 = bf16[256,1024]{1,0:T(8,128)(2,1)S(1)} copy-done((bf16[256,1024]{1,0:T(8,128)(2,1)S(1)}, bf16[256,1024]{1,0:T(8,128)(2,1)}, u32[]{:S(2)}) %copy-start.4) | copy-done | bytes 524312
  5.6 0.0 copy-start.5
  5.6 1.0 %copy-done.5 = bf16[256,1024]{1,0:T(8,128)(2,1)S(1)} copy-done((bf16[256,1024]{1,0:T(8,128)(2,1)S(1)}, bf16[256,1024]{1,0:T(8,128)(2,1)}, u32[]{:S(2)}) %copy-start.5) | copy-done | bytes 524312
  6.6 0.0 copy-start.6
  6.6 0.7 copy-done.6
  7.4 0.0 copy-start.7
  7.4 0.7 copy-done.7
  8.0 5.4 %shard_map.145 = (f32[4,1024,128]{2,1,0:T(8,128)}, f32[16,8,256]{2,1,0:T(8,128)S(1)}, f32[4,256,128]{2,1,0:T(8,128)S(1)}, bf16[1024,256]{1,0:T(8,128)(2,1)S(1)},...) custom-call(s32[1,256]{1,0:T(1,128)S(1)} %bitcast.6, ...), custom_call_target="tpu_custom_call" | custom-call | tf_op jit(solution)/shard_map/pallas_call | solution.py:536
  13.4 0.0 copy-start.1
  13.4 37.8 %shard_map.146 = (f32[1024,256]{1,0:T(8,128)S(1)}, f32[1024,256]{1,0:T(8,128)}, f32[16,8,256]{2,1,0:T(8,128)S(1)}, f32[4,256,128]{2,1,0:T(8,128)S(1)}, f32[4,1024,128]{2,1,0:T(8,128)}) custom-call(f32[4,1024,128]{2,1,0:T(8,128)} %get-tuple-element.26.states_ref, f32[16,128]{1,0:T(8,128)S(1)} %get-tuple-element.27.dec_ref, ...), custom_call_target="tpu_custom_call" | custom-call | tf_op jit(solution)/shard_map/pallas_call | solution.py:564
  51.2 0.0 copy-start.3
  51.2 1.0 copy-done.3
  52.2 0.0 copy-done.1
  52.2 8.2 %shard_map.147 = (bf16[256,1024]{1,0:T(8,128)(2,1)}, f32[256,1024]{1,0:T(8,128)}, f32[16,256]{1,0:T(8,128)}, f32[2560,128]{1,0:T(8,128)}) custom-call(s32[1,256]{1,0:T(1,128)S(1)} %bitcast.7, f32[16,256]{1,0:T(8,128)S(1)} %copy-done.6, f32[16,1]{1,0:T(8,128)S(1)} %copy.19.bias_ref, f32[16,1]{1,0:T(8,128)S(1)} %copy.20.dlog_ref, f32[16,1]{1,0:T(8,128)S(1)} %copy.21.gain_ref, ...), custom_call_target="tpu_custom_call" | custom-call | tf_op jit(solution)/shard_map/pallas_call | solution.py:608
  60.3 0.0 copy-start.2
  60.3 1.3 %copy-done.2 = f32[2560,128]{1,0:T(8,128)S(1)} copy-done((f32[2560,128]{1,0:T(8,128)S(1)}, f32[2560,128]{1,0:T(8,128)}, u32[]{:S(2)}) %copy-start.2) | copy-done | bytes 1310744
  61.7 34.6 %shard_map.148 = (f32[2,1024,128]{2,1,0:T(8,128)S(1)}, f32[2,5,128]{2,1,0:T(8,128)S(1)}, f32[16,128]{1,0:T(8,128)S(1)}) custom-call(f32[2560,128]{1,0:T(8,128)S(1)} %copy-done.2), custom_call_target="tpu_custom_call" | custom-call | tf_op jit(solution)/shard_map/pallas_call | solution.py:477
  96.3 0.6 copy.22
  96.9 0.7 copy.23
  97.5 1.0 copy.25
  (1 shorter events, 0.0 us)
Async XLA Ops:
  3.5 1.0 %copy-start = (bf16[256,1024]{1,0:T(8,128)(2,1)S(1)}, bf16[256,1024]{1,0:T(8,128)(2,1)}, u32[]{:S(2)}) copy-start(bf16[256,1024]{1,0:T(8,128)(2,1)} %feat_ref.3) | copy-start | bytes 1572868
  4.6 1.0 %copy-start.4 = (bf16[256,1024]{1,0:T(8,128)(2,1)S(1)}, bf16[256,1024]{1,0:T(8,128)(2,1)}, u32[]{:S(2)}) copy-start(bf16[256,1024]{1,0:T(8,128)(2,1)} %x_ref.1) | copy-start | bytes 1572868
  5.6 1.0 %copy-start.5 = (bf16[256,1024]{1,0:T(8,128)(2,1)S(1)}, bf16[256,1024]{1,0:T(8,128)(2,1)}, u32[]{:S(2)}) copy-start(bf16[256,1024]{1,0:T(8,128)(2,1)} %u_ref.1) | copy-start | bytes 1572868
  6.6 0.7 copy-start.6
  7.4 0.7 copy-start.7
  13.4 38.8 %copy-start.1 = (bf16[256,1024]{1,0:T(8,128)(2,1)S(1)}, bf16[256,1024]{1,0:T(8,128)(2,1)}, u32[]{:S(2)}) copy-start(bf16[256,1024]{1,0:T(8,128)(2,1)} %feat_ref.3) | copy-start | bytes 1572868
  51.2 1.0 copy-start.3
  60.3 1.3 %copy-start.2 = (f32[2560,128]{1,0:T(8,128)S(1)}, f32[2560,128]{1,0:T(8,128)}, u32[]{:S(2)}) copy-start(f32[2560,128]{1,0:T(8,128)} %get-tuple-element.40.part_ref) | copy-start | bytes 3932164
